TPU v7x, 256 devices: a whole 4x4x8 slice. The times are simulated.
256 devices in a mesh: sx: 8 (over z_hi, x), sy: 4 (over z_lo), af: 8 (over y, core).
Axes of the slice: x: 4, y: 4, z: 8 (z_hi: 2, z_lo: 4; z = z_hi * 4 + z_lo), core: 2. Of those that a mesh axis runs over, the one named last changes fastest.
Arguments:
- volume: bfloat16 [8, 48, 48, 48, 128], P('af', 'sx', 'sy'), may hold values from -6 to 6
- kernel: bfloat16 [3, 3, 3, 128, 256], P(None, None, None, 'sx', ('sy', 'af')), may hold values from -0.109375 to 0.109375
- cotangent: bfloat16 [8, 256, 24, 576], P('sx', ('sy', 'af')), may hold values from -6 to 6
Outputs:
- features: bfloat16 [8, 256, 24, 576], P('sx', ('sy', 'af'))
- volume_grad: bfloat16 [8, 48, 48, 48, 128], P('af', 'sx', 'sy')
- kernel_grad: float32 [3, 3, 3, 128, 256], P(None, None, None, 'sx', ('sy', 'af'))
All inputs are finite; a program needn't handle non-finite values.
Results may differ from a plain program's by a relative error of at most 0.0025.
Values may be sent and summed in bfloat16 or wider, within the bound.
A program may use at most 64 MiB of HBM per device.

v0:
```python
import jax
import jax.numpy as jnp
from jax import lax
from jax.sharding import PartitionSpec as P


def from_behind(value, axis, steps):
    count = lax.axis_size(axis)
    leading, last = (max(0, -steps), min(count, count - steps))
    return lax.ppermute(value, axis, [(source, source + steps) for source in range(leading, last)])


def strided_patch(extended, tap_d, tap_h, tap_w, depth, height, width):
    return extended[
        :,
        tap_d : tap_d + 2 * depth : 2,
        tap_h : tap_h + 2 * height : 2,
        tap_w : tap_w + 2 * width : 2,
        :,
    ]


def weave(even_part, odd_part, axis):
    stacked = jnp.stack([even_part, odd_part], axis=axis + 1)
    shape = list(even_part.shape)
    shape[axis] = shape[axis] * 2
    return stacked.reshape(shape)


def spread_back(grad_space, kernel_full):
    samples, depth, height, width, filters = grad_space.shape
    channels = kernel_full.shape[3]
    grad_flat = grad_space.reshape(-1, filters)
    classes = {}
    for tap_d in range(3):
        for tap_h in range(3):
            for tap_w in range(3):
                term = lax.dot_general(
                    grad_flat,
                    kernel_full[tap_d, tap_h, tap_w],
                    (((1,), (1,)), ((), ())),
                    preferred_element_type=jnp.float32,
                )
                term = term.reshape(samples, depth, height, width, channels)
                pads = [(0, 0)]
                for tap in (tap_d, tap_h, tap_w):
                    pads.append((1, 0) if tap == 2 else (0, 1))
                pads.append((0, 0))
                term = jnp.pad(term, pads)
                key_name = (tap_d % 2, tap_h % 2, tap_w % 2)
                classes[key_name] = classes[key_name] + term if key_name in classes else term
    planes = []
    for parity_d in range(2):
        rows_h = []
        for parity_h in range(2):
            rows_h.append(weave(classes[parity_d, parity_h, 0], classes[parity_d, parity_h, 1], 3))
        planes.append(weave(rows_h[0], rows_h[1], 2))
    whole = weave(planes[0], planes[1], 1)
    return whole[:, : 2 * depth + 1, : 2 * height + 1, : 2 * width + 1, :]


def on_device(volume, kernel, cotangent):
    samples = volume.shape[0]
    depth = volume.shape[1] // 2
    height = volume.shape[2] // 2
    width = volume.shape[3] // 2
    n_sy = lax.axis_size("sy")
    n_af = lax.axis_size("af")
    kernel_part = lax.all_gather(kernel, ("sy", "af"), axis=4, tiled=True)
    kernel_full = lax.all_gather(kernel_part, "sx", axis=3, tiled=True)
    filters = kernel_full.shape[4]
    per_dev = filters // (n_sy * n_af)
    below = from_behind(volume[:, -1:], "sx", 1)
    extended = jnp.concatenate([below, volume], axis=1)
    beside = from_behind(extended[:, :, -1:], "sy", 1)
    extended = jnp.concatenate([beside, extended], axis=2)
    extended = jnp.pad(extended, ((0, 0), (0, 0), (0, 0), (1, 0), (0, 0)))
    rows = samples * depth * height * width
    total = jnp.zeros((rows, filters), jnp.float32)
    for tap_d in range(3):
        for tap_h in range(3):
            for tap_w in range(3):
                patch = strided_patch(extended, tap_d, tap_h, tap_w, depth, height, width).reshape(
                    rows, -1
                )
                total = total + jnp.dot(
                    patch, kernel_full[tap_d, tap_h, tap_w], preferred_element_type=jnp.float32
                )
    conv_space = total.astype(jnp.bfloat16).reshape(
        samples, depth, height, width, n_sy, n_af, per_dev
    )
    by_sample = lax.all_to_all(conv_space, "af", split_axis=5, concat_axis=0, tiled=True)
    gathered = lax.all_to_all(
        lax.all_to_all(by_sample, "sx", split_axis=0, concat_axis=1, tiled=True),
        "sy",
        split_axis=4,
        concat_axis=2,
        tiled=True,
    )
    own_samples = gathered.shape[0]
    edge_d = gathered.shape[1]
    edge_h = gathered.shape[2]
    features = (
        gathered.reshape(own_samples, edge_d, edge_h, width, per_dev)
        .transpose(0, 4, 1, 2, 3)
        .reshape(own_samples, per_dev, edge_d, edge_h * width)
    )
    grad_after = (
        cotangent.reshape(own_samples, per_dev, edge_d, edge_h, width)
        .transpose(0, 2, 3, 4, 1)
        .reshape(own_samples, edge_d, edge_h, width, 1, 1, per_dev)
    )
    grad_region = lax.all_to_all(
        lax.all_to_all(grad_after, "sx", split_axis=1, concat_axis=0, tiled=True),
        "sy",
        split_axis=2,
        concat_axis=4,
        tiled=True,
    )
    grad_back = lax.all_to_all(grad_region, "af", split_axis=0, concat_axis=5, tiled=True)
    grad_space = grad_back.reshape(samples, depth, height, width, filters)
    grad_flat = grad_space.reshape(rows, filters)
    tap_grads = []
    for tap_d in range(3):
        for tap_h in range(3):
            for tap_w in range(3):
                patch = strided_patch(extended, tap_d, tap_h, tap_w, depth, height, width).reshape(
                    rows, -1
                )
                tap_grads.append(
                    lax.dot_general(
                        patch,
                        grad_flat,
                        (((0,), (0,)), ((), ())),
                        preferred_element_type=jnp.float32,
                    )
                )
    kernel_terms = jnp.stack(tap_grads, axis=0).reshape(3, 3, 3, kernel_full.shape[3], filters)
    reduced = lax.psum_scatter(kernel_terms, ("sy", "af"), scatter_dimension=4, tiled=True)
    kernel_grad = lax.psum_scatter(reduced, "sx", scatter_dimension=3, tiled=True)
    partial_grad = spread_back(grad_space, kernel_full)
    from_above = from_behind(partial_grad[:, 0:1], "sx", -1)
    own_depth = partial_grad[:, 1:]
    own_depth = jnp.concatenate([own_depth[:, :-1], own_depth[:, -1:] + from_above], axis=1)
    from_right = from_behind(own_depth[:, :, 0:1].astype(jnp.bfloat16), "sy", -1).astype(
        jnp.float32
    )
    own_height = own_depth[:, :, 1:]
    own_height = jnp.concatenate(
        [own_height[:, :, :-1], own_height[:, :, -1:] + from_right], axis=2
    )
    volume_grad = own_height[:, :, :, 1:]
    return (features, volume_grad.astype(jnp.bfloat16), kernel_grad)


def solution(mesh):
    return jax.shard_map(
        on_device,
        mesh=mesh,
        in_specs=(
            P("af", "sx", "sy", None, None),
            P(None, None, None, "sx", ("sy", "af")),
            P("sx", ("sy", "af"), None, None),
        ),
        out_specs=(
            P("sx", ("sy", "af"), None, None),
            P("af", "sx", "sy", None, None),
            P(None, None, None, "sx", ("sy", "af")),
        ),
        check_vma=False,
    )
```

profile of v0, /device:TPU:8, one launch (start us, length us, event | category | flops | bytes accessed | tf_op | source)
XLA Modules:
  0.0 482.0 jit_solution(499693870692736997)
XLA Ops:
  10.8 2.2 reshape.377
  13.1 10.9 %all-to-all-start.3 = ((bf16[8,2,6912]{2,1,0:T(2,128)(2,1)}), bf16[8,2,6912]{2,1,0:T(2,128)(2,1)S(1)}, u32[]{:S(2)}, u32[]{:S(2)}) async-start(bf16[8,2,6912]{2,1,0:T(2,128)(2,1)} %reshape.377), calls=%async_computation.3 | async-start | bytes 442368 | tf_op jit(solution)/shard_map/all_to_all | solution.py:114
  24.9 3.9 collective-permute-start
  28.9 6.1 %all-to-all-done.3 = bf16[8,2,6912]{2,1,0:T(2,128)(2,1)S(1)} async-done(((bf16[8,2,6912]{2,1,0:T(2,128)(2,1)}), bf16[8,2,6912]{2,1,0:T(2,128)(2,1)S(1)}, u32[]{:S(2)}, u32[]{:S(2)}) %all-to-all-start.3) | async-done | bytes 221216 | tf_op jit(solution)/shard_map/all_to_all | solution.py:114
  37.0 2.2 reshape.379
  39.2 4.9 %all-to-all-start.4 = ((bf16[4,2,13824]{2,1,0:T(2,128)(2,1)}), bf16[4,2,13824]{2,1,0:T(2,128)(2,1)S(1)}, u32[]{:S(2)}, u32[]{:S(2)}) async-start(bf16[4,2,13824]{2,1,0:T(2,128)(2,1)} %reshape.379), calls=%async_computation.4 | async-start | bytes 442368 | tf_op jit(solution)/shard_map/all_to_all | solution.py:113
  44.9 3.9 collective-permute-start.1
  52.5 2.2 reshape.381
  54.8 4.9 %all-to-all-start.5 = ((bf16[8,2,6912]{2,1,0:T(2,128)(2,1)}), bf16[8,2,6912]{2,1,0:T(2,128)(2,1)S(1)}, u32[]{:S(2)}, u32[]{:S(2)}) async-start(bf16[8,2,6912]{2,1,0:T(2,128)(2,1)} %reshape.381), calls=%async_computation.5 | async-start | bytes 442368 | tf_op jit(solution)/shard_map/all_to_all | solution.py:120
  59.7 42.8 %all_gather.6 = bf16[3,3,3,16,256]{3,4,2,1,0:T(8,128)(2,1)S(1)} all-gather(bf16[3,3,3,16,8]{3,4,2,1,0:T(8,128)(2,1)S(1)} %copy-done.50), channel_id=1, replica_groups=mesh['sx'=8,'sy'=4,'af'=8] {'sy','af'}, dimensions={4}, use_global_device_ids=true | all-gather | bytes 228096 | tf_op jit(solution)/shard_map/all_gather | solution.py:69
  104.5 5.5 %slice.257 = bf16[1,3,6,24,128]{4,3,2,1,0:T(8,128)(2,1)} slice(bf16[1,7,13,49,128]{4,3,2,1,0:T(8,128)(2,1)S(1)} %fusion.3), slice={[0:1:1], [0:6:2], [0:12:2], [0:48:2], [0:128:1]} | slice | bytes 221184 | tf_op jit(solution)/shard_map/slice | solution.py:14
  112.1 5.5 %slice.267 = bf16[1,3,6,24,128]{4,3,2,1,0:T(8,128)(2,1)} slice(bf16[1,7,13,49,128]{4,3,2,1,0:T(8,128)(2,1)S(1)} %fusion.3), slice={[0:1:1], [0:6:2], [1:13:2], [2:49:2], [0:128:1]} | slice | bytes 221184 | tf_op jit(solution)/shard_map/slice | solution.py:14
  117.6 5.5 %slice.269 = bf16[1,3,6,24,128]{4,3,2,1,0:T(8,128)(2,1)} slice(bf16[1,7,13,49,128]{4,3,2,1,0:T(8,128)(2,1)S(1)} %fusion.3), slice={[0:1:1], [0:6:2], [2:13:2], [0:48:2], [0:128:1]} | slice | bytes 221184 | tf_op jit(solution)/shard_map/slice | solution.py:14
  123.1 5.5 %slice.271 = bf16[1,3,6,24,128]{4,3,2,1,0:T(8,128)(2,1)} slice(bf16[1,7,13,49,128]{4,3,2,1,0:T(8,128)(2,1)S(1)} %fusion.3), slice={[0:1:1], [0:6:2], [2:13:2], [1:49:2], [0:128:1]} | slice | bytes 221184 | tf_op jit(solution)/shard_map/slice | solution.py:14
  128.6 5.5 %slice.273 = bf16[1,3,6,24,128]{4,3,2,1,0:T(8,128)(2,1)} slice(bf16[1,7,13,49,128]{4,3,2,1,0:T(8,128)(2,1)S(1)} %fusion.3), slice={[0:1:1], [0:6:2], [2:13:2], [2:49:2], [0:128:1]} | slice | bytes 221184 | tf_op jit(solution)/shard_map/slice | solution.py:14
  134.1 5.5 %slice.275 = bf16[1,3,6,24,128]{4,3,2,1,0:T(8,128)(2,1)} slice(bf16[1,7,13,49,128]{4,3,2,1,0:T(8,128)(2,1)S(1)} %fusion.3), slice={[0:1:1], [1:7:2], [0:12:2], [0:48:2], [0:128:1]} | slice | bytes 221184 | tf_op jit(solution)/shard_map/slice | solution.py:14
  139.6 5.4 %slice.277 = bf16[1,3,6,24,128]{4,3,2,1,0:T(8,128)(2,1)} slice(bf16[1,7,13,49,128]{4,3,2,1,0:T(8,128)(2,1)S(1)} %fusion.3), slice={[0:1:1], [1:7:2], [0:12:2], [1:49:2], [0:128:1]} | slice | bytes 221184 | tf_op jit(solution)/shard_map/slice | solution.py:14
  145.0 5.5 %slice.279 = bf16[1,3,6,24,128]{4,3,2,1,0:T(8,128)(2,1)} slice(bf16[1,7,13,49,128]{4,3,2,1,0:T(8,128)(2,1)S(1)} %fusion.3), slice={[0:1:1], [1:7:2], [0:12:2], [2:49:2], [0:128:1]} | slice | bytes 221184 | tf_op jit(solution)/shard_map/slice | solution.py:14
  150.5 5.5 %slice.281 = bf16[1,3,6,24,128]{4,3,2,1,0:T(8,128)(2,1)} slice(bf16[1,7,13,49,128]{4,3,2,1,0:T(8,128)(2,1)S(1)} %fusion.3), slice={[0:1:1], [1:7:2], [1:13:2], [0:48:2], [0:128:1]} | slice | bytes 221184 | tf_op jit(solution)/shard_map/slice | solution.py:14
  156.0 5.5 %slice.283 = bf16[1,3,6,24,128]{4,3,2,1,0:T(8,128)(2,1)} slice(bf16[1,7,13,49,128]{4,3,2,1,0:T(8,128)(2,1)S(1)} %fusion.3), slice={[0:1:1], [1:7:2], [1:13:2], [1:49:2], [0:128:1]} | slice | bytes 221184 | tf_op jit(solution)/shard_map/slice | solution.py:14
  161.4 5.5 %slice.285 = bf16[1,3,6,24,128]{4,3,2,1,0:T(8,128)(2,1)} slice(bf16[1,7,13,49,128]{4,3,2,1,0:T(8,128)(2,1)S(1)} %fusion.3), slice={[0:1:1], [1:7:2], [1:13:2], [2:49:2], [0:128:1]} | slice | bytes 221184 | tf_op jit(solution)/shard_map/slice | solution.py:14
  166.9 5.5 %slice.287 = bf16[1,3,6,24,128]{4,3,2,1,0:T(8,128)(2,1)} slice(bf16[1,7,13,49,128]{4,3,2,1,0:T(8,128)(2,1)S(1)} %fusion.3), slice={[0:1:1], [1:7:2], [2:13:2], [0:48:2], [0:128:1]} | slice | bytes 221184 | tf_op jit(solution)/shard_map/slice | solution.py:14
  172.4 5.5 %slice.289 = bf16[1,3,6,24,128]{4,3,2,1,0:T(8,128)(2,1)} slice(bf16[1,7,13,49,128]{4,3,2,1,0:T(8,128)(2,1)S(1)} %fusion.3), slice={[0:1:1], [1:7:2], [2:13:2], [1:49:2], [0:128:1]} | slice | bytes 221184 | tf_op jit(solution)/shard_map/slice | solution.py:14
  177.9 5.6 %slice.291 = bf16[1,3,6,24,128]{4,3,2,1,0:T(8,128)(2,1)} slice(bf16[1,7,13,49,128]{4,3,2,1,0:T(8,128)(2,1)S(1)} %fusion.3), slice={[0:1:1], [1:7:2], [2:13:2], [2:49:2], [0:128:1]} | slice | bytes 221184 | tf_op jit(solution)/shard_map/slice | solution.py:14
  183.5 5.5 %slice.293 = bf16[1,3,6,24,128]{4,3,2,1,0:T(8,128)(2,1)} slice(bf16[1,7,13,49,128]{4,3,2,1,0:T(8,128)(2,1)S(1)} %fusion.3), slice={[0:1:1], [2:7:2], [0:12:2], [0:48:2], [0:128:1]} | slice | bytes 221184 | tf_op jit(solution)/shard_map/slice | solution.py:14
  188.9 5.5 %slice.295 = bf16[1,3,6,24,128]{4,3,2,1,0:T(8,128)(2,1)} slice(bf16[1,7,13,49,128]{4,3,2,1,0:T(8,128)(2,1)S(1)} %fusion.3), slice={[0:1:1], [2:7:2], [0:12:2], [1:49:2], [0:128:1]} | slice | bytes 221184 | tf_op jit(solution)/shard_map/slice | solution.py:14
  196.0 5.5 %slice.303 = bf16[1,3,6,24,128]{4,3,2,1,0:T(8,128)(2,1)} slice(bf16[1,7,13,49,128]{4,3,2,1,0:T(8,128)(2,1)S(1)} %fusion.3), slice={[0:1:1], [2:7:2], [1:13:2], [2:49:2], [0:128:1]} | slice | bytes 221184 | tf_op jit(solution)/shard_map/slice | solution.py:14
  201.5 5.5 %slice.305 = bf16[1,3,6,24,128]{4,3,2,1,0:T(8,128)(2,1)} slice(bf16[1,7,13,49,128]{4,3,2,1,0:T(8,128)(2,1)S(1)} %fusion.3), slice={[0:1:1], [2:7:2], [2:13:2], [0:48:2], [0:128:1]} | slice | bytes 221184 | tf_op jit(solution)/shard_map/slice | solution.py:14
  207.0 5.5 %slice.307 = bf16[1,3,6,24,128]{4,3,2,1,0:T(8,128)(2,1)} slice(bf16[1,7,13,49,128]{4,3,2,1,0:T(8,128)(2,1)S(1)} %fusion.3), slice={[0:1:1], [2:7:2], [2:13:2], [1:49:2], [0:128:1]} | slice | bytes 221184 | tf_op jit(solution)/shard_map/slice | solution.py:14
  212.5 5.5 %slice.309 = bf16[1,3,6,24,128]{4,3,2,1,0:T(8,128)(2,1)} slice(bf16[1,7,13,49,128]{4,3,2,1,0:T(8,128)(2,1)S(1)} %fusion.3), slice={[0:1:1], [2:7:2], [2:13:2], [2:49:2], [0:128:1]} | slice | bytes 221184 | tf_op jit(solution)/shard_map/slice | solution.py:14
  221.4 2.2 reshape_reshape.4
  232.6 5.3 %copy.228 = f32[3,3,3,128,256]{3,4,2,1,0:T(8,128)} copy(f32[3,3,3,128,256]{4,3,2,1,0:T(8,128)} %bitcast.680) | data formatting | bytes 7077888 | tf_op jit(solution)/shard_map/reshape | solution.py:138
  266.7 3.6 reshape.371
  270.4 8.4 %all-to-all-start = ((bf16[8,2,6912]{2,1,0:T(2,128)(2,1)}), bf16[8,2,6912]{2,1,0:T(2,128)(2,1)S(1)}, u32[]{:S(2)}, u32[]{:S(2)}) async-start(bf16[8,2,6912]{2,1,0:T(2,128)(2,1)} %reshape.371), calls=%async_computation | async-start | bytes 442368 | tf_op jit(solution)/shard_map/all_to_all | solution.py:92
  284.4 2.8 reshape.372
  287.2 2.6 fusion.194
  289.8 3.5 reshape.373
  293.3 6.5 %all-to-all-start.1 = ((bf16[8,2,6912]{2,1,0:T(2,128)(2,1)}), bf16[8,2,6912]{2,1,0:T(2,128)(2,1)S(1)}, u32[]{:S(2)}, u32[]{:S(2)}) async-start(bf16[8,2,6912]{2,1,0:T(2,128)(2,1)} %reshape.373), calls=%async_computation.1 | async-start | bytes 442368 | tf_op jit(solution)/shard_map/all_to_all | solution.py:94
  299.8 2.1 slice_add_fusion
  305.2 5.6 %all-to-all-done.1 = bf16[8,2,6912]{2,1,0:T(2,128)(2,1)S(1)} async-done(((bf16[8,2,6912]{2,1,0:T(2,128)(2,1)}), bf16[8,2,6912]{2,1,0:T(2,128)(2,1)S(1)}, u32[]{:S(2)}, u32[]{:S(2)}) %all-to-all-start.1) | async-done | bytes 221216 | tf_op jit(solution)/shard_map/all_to_all | solution.py:94
  310.8 2.7 reshape.374
  313.5 2.5 copy_bitcast_fusion.2
  316.0 3.5 reshape.375
  319.5 3.4 all-to-all-start.2
  323.0 62.4 %reduce-scatter.5.cloned.1.call-done = f32[3,3,3,128,8]{3,4,2,1,0:T(8,128)} async-done(((f32[3,3,3,128,256]{3,4,2,1,0:T(8,128)}), f32[3,3,3,128,8]{3,4,2,1,0:T(8,128)}) %reduce-scatter.5.cloned.1.call-update) | async-done | bytes 110608 | tf_op jit(solution)/shard_map/reduce_scatter | solution.py:139
  385.4 3.1 copy.284
  388.5 3.4 reshape.369
  397.9 74.8 %reduce-scatter.7.cloned.1.call-done = f32[16,216]{1,0:T(8,128)} async-done(((f32[128,216]{1,0:T(8,128)}), f32[16,216]{1,0:T(8,128)}) %reduce-scatter.7.cloned.1.call-update) | async-done | bytes 13840
  (259 shorter events, 72.1 us)
Async XLA Ops:
  13.1 21.9 %all-to-all-start.3 = ((bf16[8,2,6912]{2,1,0:T(2,128)(2,1)}), bf16[8,2,6912]{2,1,0:T(2,128)(2,1)S(1)}, u32[]{:S(2)}, u32[]{:S(2)}) async-start(bf16[8,2,6912]{2,1,0:T(2,128)(2,1)} %reshape.377), calls=%async_computation.3 | async-start | bytes 442368 | tf_op jit(solution)/shard_map/all_to_all | solution.py:114
  24.9 19.2 %collective-permute-start = (bf16[1,1,12,48,128]{4,3,2,1,0:T(8,128)(2,1)S(1)}, bf16[1,1,12,48,128]{4,3,2,1,0:T(8,128)(2,1)S(1)}, u32[]{:S(2)}, u32[]{:S(2)}) collective-permute-start(bf16[1,1,12,48,128]{4,3,2,1,0:T(8,128)(2,1)S(1)} %slice.255), channel_id=1, source_target_pairs={{0,32},{32,64},{64,96},{96,128},{128,160},{160,192},{192,224},{1,3... | collective-permute-start | bytes 442376 | tf_op jit(solution)/shard_map/ppermute | solution.py:10
  37.0 7.2 %copy-start.5 = (bf16[1,6,12,48,128]{4,3,2,1,0:T(8,128)(2,1)S(1)}, bf16[1,6,12,48,128]{4,3,2,1,0:T(8,128)(2,1)}, u32[]{:S(2)}) copy-start(bf16[1,6,12,48,128]{4,3,2,1,0:T(8,128)(2,1)} %param.3) | copy-start | bytes 2654212
  39.2 11.3 %all-to-all-start.4 = ((bf16[4,2,13824]{2,1,0:T(2,128)(2,1)}), bf16[4,2,13824]{2,1,0:T(2,128)(2,1)S(1)}, u32[]{:S(2)}, u32[]{:S(2)}) async-start(bf16[4,2,13824]{2,1,0:T(2,128)(2,1)} %reshape.379), calls=%async_computation.4 | async-start | bytes 442368 | tf_op jit(solution)/shard_map/all_to_all | solution.py:113
  44.9 59.2 %collective-permute-start.1 = (bf16[1,7,1,48,128]{4,3,2,1,0:T(8,128)(2,1)}, bf16[1,7,1,48,128]{4,3,2,1,0:T(8,128)(2,1)S(1)}, u32[]{:S(2)}, u32[]{:S(2)}) collective-permute-start(bf16[1,7,1,48,128]{4,3,2,1,0:T(8,128)(2,1)} %slice.318), channel_id=1, source_target_pairs={{0,8},{8,16},{16,24},{1,9},{9,17},{17,25},{2,10},{10,18},{18,26},{... | collective-permute-start | bytes 258056 | tf_op jit(solution)/shard_map/ppermute | solution.py:10
  52.2 7.5 %copy-start.50 = (bf16[3,3,3,16,8]{3,4,2,1,0:T(8,128)(2,1)S(1)}, bf16[3,3,3,16,8]{3,4,2,1,0:T(8,128)(2,1)}, u32[]{:S(2)}) copy-start(bf16[3,3,3,16,8]{3,4,2,1,0:T(8,128)(2,1)} %param.4) | copy-start | bytes 20740
  54.8 163.3 %all-to-all-start.5 = ((bf16[8,2,6912]{2,1,0:T(2,128)(2,1)}), bf16[8,2,6912]{2,1,0:T(2,128)(2,1)S(1)}, u32[]{:S(2)}, u32[]{:S(2)}) async-start(bf16[8,2,6912]{2,1,0:T(2,128)(2,1)} %reshape.381), calls=%async_computation.5 | async-start | bytes 442368 | tf_op jit(solution)/shard_map/all_to_all | solution.py:120
  59.7 178.3 %all-gather.2.cloned.1.call-start = ((), (), s32[]{:S(2)}) async-start(), calls=%async_computation.8 | async-start | bytes 1990656 | tf_op jit(solution)/shard_map/all_gather | solution.py:70
  103.8 281.5 %reduce-scatter.5.cloned.1.call-start = ((), (), s32[]{:S(2)}) async-start(), calls=%async_computation.9 | async-start | bytes 3649536 | tf_op jit(solution)/shard_map/reduce_scatter | solution.py:139
  112.1 112.6 %copy-start.8 = (bf16[1,3,6,24,128]{4,3,2,1,0:T(8,128)(2,1)}, bf16[1,3,6,24,128]{4,3,2,1,0:T(8,128)(2,1)S(1)}, u32[]{:S(2)}) copy-start(bf16[1,3,6,24,128]{4,3,2,1,0:T(8,128)(2,1)S(1)} %slice.265) | copy-start | bytes 331780
  195.4 33.9 %copy-start.6 = (bf16[1,3,6,24,128]{4,3,2,1,0:T(8,128)(2,1)}, bf16[1,3,6,24,128]{4,3,2,1,0:T(8,128)(2,1)S(1)}, u32[]{:S(2)}) copy-start(bf16[1,3,6,24,128]{4,3,2,1,0:T(8,128)(2,1)S(1)} %slice.299) | copy-start | bytes 331780
  195.9 33.7 %copy-start.10 = (bf16[1,3,6,24,128]{4,3,2,1,0:T(8,128)(2,1)}, bf16[1,3,6,24,128]{4,3,2,1,0:T(8,128)(2,1)S(1)}, u32[]{:S(2)}) copy-start(bf16[1,3,6,24,128]{4,3,2,1,0:T(8,128)(2,1)S(1)} %slice.301) | copy-start | bytes 331780
  219.8 3.8 copy-start.48
  221.4 3.5 copy-start.12
  223.6 1.5 copy-start.15
  223.6 1.8 copy-start.19
  223.9 1.8 copy-start.23
  224.1 1.8 copy-start.27
  224.4 1.8 copy-start.29
  224.6 1.8 copy-start.31
  224.9 1.8 copy-start.33
  225.2 1.8 copy-start.35
  227.2 1.4 copy-start.45
  227.5 1.3 copy-start.47
  228.1 1.8 copy-start.14
  228.3 1.8 copy-start.17
  228.6 1.7 copy-start.21
  228.9 1.7 copy-start.25
  230.8 1.8 copy-start.4
  238.0 2.7 copy-start.1
  257.1 1.5 copy-start.38
  257.1 1.7 copy-start.36
  257.1 1.9 copy-start.34
  258.3 1.3 copy-start.28
  258.6 1.3 copy-start.24
  258.8 1.3 copy-start.20
  259.5 1.3 copy-start.9
  260.3 1.7 copy-start.26
  260.5 1.7 copy-start.22
  260.8 1.7 copy-start.18
  266.7 12.0 %copy-start.2 = (f32[1,4,7,2,50,128]{5,1,4,3,2,0:T(4,128)S(1)}, f32[1,4,7,2,50,128]{5,1,4,3,2,0:T(4,128)}, u32[]{:S(2)}) copy-start(f32[1,4,7,2,50,128]{5,1,4,3,2,0:T(4,128)} %copy.225) | copy-start | bytes 4300804
  270.4 14.1 %all-to-all-start = ((bf16[8,2,6912]{2,1,0:T(2,128)(2,1)}), bf16[8,2,6912]{2,1,0:T(2,128)(2,1)S(1)}, u32[]{:S(2)}, u32[]{:S(2)}) async-start(bf16[8,2,6912]{2,1,0:T(2,128)(2,1)} %reshape.371), calls=%async_computation | async-start | bytes 442368 | tf_op jit(solution)/shard_map/all_to_all | solution.py:92
  280.9 1.6 copy-start
  281.0 18.8 %collective-permute-start.2 = (f32[1,1,13,49,128]{4,1,3,2,0:T(1,128)S(1)}, f32[1,1,13,49,128]{4,1,3,2,0:T(1,128)S(1)}, u32[]{:S(2)}, u32[]{:S(2)}) collective-permute-start(f32[1,1,13,49,128]{4,1,3,2,0:T(1,128)S(1)} %slice.348), channel_id=1, source_target_pairs={{32,0},{64,32},{96,64},{128,96},{160,128},{192,160},{224,192},{33,... | collective-permute-start | bytes 978440 | tf_op jit(solution)/shard_map/ppermute | solution.py:10
  293.3 17.4 %all-to-all-start.1 = ((bf16[8,2,6912]{2,1,0:T(2,128)(2,1)}), bf16[8,2,6912]{2,1,0:T(2,128)(2,1)S(1)}, u32[]{:S(2)}, u32[]{:S(2)}) async-start(bf16[8,2,6912]{2,1,0:T(2,128)(2,1)} %reshape.373), calls=%async_computation.1 | async-start | bytes 442368 | tf_op jit(solution)/shard_map/all_to_all | solution.py:94
  303.7 88.3 %collective-permute-start.3 = (bf16[1,6,1,49,128]{4,1,3,2,0:T(8,128)(2,1)S(1)}, bf16[1,6,1,49,128]{4,1,3,2,0:T(8,128)(2,1)S(1)}, u32[]{:S(2)}, u32[]{:S(2)}) collective-permute-start(bf16[1,6,1,49,128]{4,1,3,2,0:T(8,128)(2,1)S(1)} %slice.352), channel_id=1, source_target_pairs={{8,0},{16,8},{24,16},{9,1},{17,9},{25,17},{10,2},{18,10},{26,18},{... | collective-permute-start | bytes 225800 | tf_op jit(solution)/shard_map/ppermute | solution.py:10
  319.5 75.0 %all-to-all-start.2 = ((bf16[4,2,13824]{2,1,0:T(2,128)(2,1)}), bf16[4,2,13824]{2,1,0:T(2,128)(2,1)S(1)}, u32[]{:S(2)}, u32[]{:S(2)}) async-start(bf16[4,2,13824]{2,1,0:T(2,128)(2,1)} %reshape.375), calls=%async_computation.2 | async-start | bytes 442368 | tf_op jit(solution)/shard_map/all_to_all | solution.py:93
  322.9 149.8 %reduce-scatter.7.cloned.1.call-start = ((), (), s32[]{:S(2)}) async-start(), calls=%async_computation.10 | async-start | bytes 147456
  (17 other events, 19.2 us)
Sparse Core Ops, SparseCore 0:
  104.0 68.6 all-gather.1
  392.1 80.5 reduce-scatter.6
Sparse Core Ops, SparseCore 1:
  238.1 147.2 reduce-scatter.4
where the time goes:
time: 491 us; the launch traced here: 482 us
  local copies, waits for them, and re-layouts  187 us (38%)
  waiting for transfers between devices  152 us (31%)
  starting transfers between devices  49.8 us (10%)
  blocking collectives  42.8 us (9%)
  matrix products  26.6 us (5%)
  between operations  17.2 us (4%)
  other arithmetic  5.71 us (1%)
    slice x27, local copies, waits for them, and re-layouts, strided_patch(): extended[:, tap_d:tap_d + 2 * depth:2, tap_h:tap_h + 2 * height:2, tap_w:...  113 us
    unnamed x4, waiting for transfers between devices  74.9 us
    reduce_scatter x1, waiting for transfers between devices, on_device(): lax.psum_scatter(kernel_terms, ('sy', 'af'), scatter_dimension=4, tiled=T...  62.4 us
    unnamed x122, local copies, waits for them, and re-layouts  47.6 us
    all_gather x1, blocking collectives, on_device(): kernel_part = lax.all_gather(kernel, ('sy', 'af'), axis=4, tiled=True)  42.8 us
    dot_general x27, matrix products, spread_back(): lax.dot_general(grad_flat, kernel_full[tap_d, tap_h, tap_w], (((1,), (1,)...  14.2 us
    all_to_all x1, starting transfers between devices, on_device(): lax.all_to_all(grad_after, 'sx', split_axis=1, concat_axis=0, tiled=True)  10.9 us
    ppermute x4, starting transfers between devices, from_behind(): lax.ppermute(value, axis, [(source, source + steps) for source in range(l...  10.6 us
  transfers between devices with their start and end apart: 13, of which 6 were waited for; matrix products, arithmetic and copies ran while one was open for 43% of the time, Pallas kernels for 0%

commit v1 on v0

--- a/solution.py
+++ b/solution.py
@@ -18,6 +18,26 @@
         tap_w : tap_w + 2 * width : 2,
         :,
     ]
+
+
+def parity_view(extended):
+    samples, d_ext, h_ext, w_ext, channels = extended.shape
+    pads = [(0, 0)] + [(0, n % 2) for n in (d_ext, h_ext, w_ext)] + [(0, 0)]
+    even = jnp.pad(extended, pads)
+    _, d2, h2, w2, _ = even.shape
+    split = even.reshape(samples, d2 // 2, 2, h2 // 2, 2, w2 // 2, 2, channels)
+    return split.transpose(2, 4, 6, 0, 1, 3, 5, 7)
+
+
+def im2col(classes, depth, height, width):
+    patches = []
+    for tap_d in range(3):
+        for tap_h in range(3):
+            for tap_w in range(3):
+                cls = classes[tap_d % 2, tap_h % 2, tap_w % 2]
+                od, oh, ow = tap_d // 2, tap_h // 2, tap_w // 2
+                patches.append(cls[:, od : od + depth, oh : oh + height, ow : ow + width, :])
+    return jnp.concatenate(patches, axis=-1)
 
 
 def weave(even_part, odd_part, axis):
@@ -76,16 +96,10 @@
     extended = jnp.concatenate([beside, extended], axis=2)
     extended = jnp.pad(extended, ((0, 0), (0, 0), (0, 0), (1, 0), (0, 0)))
     rows = samples * depth * height * width
-    total = jnp.zeros((rows, filters), jnp.float32)
-    for tap_d in range(3):
-        for tap_h in range(3):
-            for tap_w in range(3):
-                patch = strided_patch(extended, tap_d, tap_h, tap_w, depth, height, width).reshape(
-                    rows, -1
-                )
-                total = total + jnp.dot(
-                    patch, kernel_full[tap_d, tap_h, tap_w], preferred_element_type=jnp.float32
-                )
+    classes = parity_view(extended)
+    cols = im2col(classes, depth, height, width).reshape(rows, -1)
+    kernel_mat = kernel_full.reshape(-1, filters)
+    total = jnp.dot(cols, kernel_mat, preferred_element_type=jnp.float32)
     conv_space = total.astype(jnp.bfloat16).reshape(
         samples, depth, height, width, n_sy, n_af, per_dev
     )
@@ -120,24 +134,17 @@
     grad_back = lax.all_to_all(grad_region, "af", split_axis=0, concat_axis=5, tiled=True)
     grad_space = grad_back.reshape(samples, depth, height, width, filters)
     grad_flat = grad_space.reshape(rows, filters)
-    tap_grads = []
-    for tap_d in range(3):
-        for tap_h in range(3):
-            for tap_w in range(3):
-                patch = strided_patch(extended, tap_d, tap_h, tap_w, depth, height, width).reshape(
-                    rows, -1
-                )
-                tap_grads.append(
-                    lax.dot_general(
-                        patch,
-                        grad_flat,
-                        (((0,), (0,)), ((), ())),
-                        preferred_element_type=jnp.float32,
-                    )
-                )
-    kernel_terms = jnp.stack(tap_grads, axis=0).reshape(3, 3, 3, kernel_full.shape[3], filters)
-    reduced = lax.psum_scatter(kernel_terms, ("sy", "af"), scatter_dimension=4, tiled=True)
-    kernel_grad = lax.psum_scatter(reduced, "sx", scatter_dimension=3, tiled=True)
+    kernel_terms = lax.dot_general(
+        cols, grad_flat, (((0,), (0,)), ((), ())), preferred_element_type=jnp.float32
+    )
+    n_sx = lax.axis_size("sx")
+    channels = kernel_full.shape[3]
+    taps = kernel_terms.reshape(27, channels, n_sy * n_af, per_dev).transpose(2, 0, 1, 3)
+    by_filter = lax.all_to_all(taps, ("sy", "af"), 0, 0, tiled=True).sum(axis=0)
+    own_ch = channels // n_sx
+    by_filter = by_filter.reshape(27, n_sx, own_ch, per_dev).transpose(1, 0, 2, 3)
+    kernel_grad = lax.all_to_all(by_filter, "sx", 0, 0, tiled=True).sum(axis=0)
+    kernel_grad = kernel_grad.reshape(3, 3, 3, own_ch, per_dev)
     partial_grad = spread_back(grad_space, kernel_full)
     from_above = from_behind(partial_grad[:, 0:1], "sx", -1)
     own_depth = partial_grad[:, 1:]

time: 491 us -> 364 us (0.74)
  local copies, waits for them, and re-layouts: 187 us -> 113 us
  waiting for transfers between devices: 152 us -> 87.8 us
  starting transfers between devices: 49.8 us -> 67.5 us
  matrix products: 26.6 us -> 18.7 us
  other arithmetic: 5.71 us -> 12.6 us
    slice x28 -> x1, local copies, waits for them, and re-layouts: 114 us -> 2.08 us  [im2col(): cls = classes[tap_d % 2, tap_h % 2, tap_w % 2]]
    unnamed x4 -> x1, waiting for transfers between devices: 74.9 us -> 0.02 us
    reduce_scatter x1 -> x0, waiting for transfers between devices: 62.4 us -> none  [on_device(): lax.psum_scatter(kernel_terms, ('sy', 'af'), scatter_dimension=4, tiled=T...]
    all_to_all x0 -> x2, waiting for transfers between devices: none -> 57.8 us  [the longest x1 54.5 us: on_device(): by_filter = lax.all_to_all(taps, ('sy', 'af'), 0, 0, tiled=True).sum(axis=0)]
    unnamed x122 -> x66, local copies, waits for them, and re-layouts: 47.6 us -> 67.3 us
    all_to_all x1, waiting for transfers between devices: 1.72 us -> 18.7 us  [on_device(): lax.all_to_all(lax.all_to_all(grad_after, 'sx', split_axis=1, concat_axis...]
    all_to_all x0 -> x2, starting transfers between devices: none -> 11.6 us  [the longest x1 7.97 us: on_device(): by_filter = lax.all_to_all(taps, ('sy', 'af'), 0, 0, tiled=True).sum(axis=0)]
    all_to_all x1, starting transfers between devices: 10.9 us -> 21.2 us  [on_device(): lax.all_to_all(grad_after, 'sx', split_axis=1, concat_axis=0, tiled=True)]
  transfers between devices with their start and end apart: 13 -> 13, of which waited for: 6 -> 5; matrix products, arithmetic and copies ran while one was open for 43% -> 31% of each run, Pallas kernels for 0% -> 0%
where the time goes in v1:
time: 364 us; the launch traced here: 357 us
  local copies, waits for them, and re-layouts  113 us (31%)
  waiting for transfers between devices  87.8 us (24%)
  starting transfers between devices  67.5 us (19%)
  blocking collectives  42.8 us (12%)
  matrix products  18.7 us (5%)
  between operations  14.8 us (4%)
  other arithmetic  12.6 us (3%)
    unnamed x66, local copies, waits for them, and re-layouts  67.3 us
    all_to_all x1, waiting for transfers between devices, on_device(): by_filter = lax.all_to_all(taps, ('sy', 'af'), 0, 0, tiled=True).sum(axis=0)  54.5 us
    all_gather x1, blocking collectives, on_device(): kernel_part = lax.all_gather(kernel, ('sy', 'af'), axis=4, tiled=True)  42.8 us
    all_to_all x1, starting transfers between devices, on_device(): lax.all_to_all(grad_after, 'sx', split_axis=1, concat_axis=0, tiled=True)  21.2 us
    all_to_all x1, waiting for transfers between devices, on_device(): lax.all_to_all(lax.all_to_all(grad_after, 'sx', split_axis=1, concat_axis...  18.7 us
    dot_general x27, matrix products, spread_back(): lax.dot_general(grad_flat, kernel_full[tap_d, tap_h, tap_w], (((1,), (1,)...  12.4 us
    ppermute x4, starting transfers between devices, from_behind(): lax.ppermute(value, axis, [(source, source + steps) for source in range(l...  10.4 us
    all_to_all x1, starting transfers between devices, on_device(): by_filter = lax.all_to_all(taps, ('sy', 'af'), 0, 0, tiled=True).sum(axis=0)  7.97 us
  transfers between devices with their start and end apart: 13, of which 5 were waited for; matrix products, arithmetic and copies ran while one was open for 31% of the time, Pallas kernels for 0%

profile of v1, /device:TPU:8, one launch (start us, length us, event | category | flops | bytes accessed | tf_op | source)
XLA Modules:
  0.0 356.9 jit_solution(4887128388619679048)
XLA Ops:
  7.2 1.8 copy.579
  9.3 3.4 collective-permute-start
  12.8 6.2 %collective-permute-done = bf16[1,1,12,48,128]{4,1,3,2,0:T(2,128)(2,1)S(1)} collective-permute-done((bf16[1,1,12,48,128]{4,1,3,2,0:T(2,128)(2,1)S(1)}, bf16[1,1,12,48,128]{4,1,3,2,0:T(2,128)(2,1)S(1)}, u32[]{:S(2)}, u32[]{:S(2)}) %collective-permute-start) | collective-permute-done | bytes 147488 | tf_op jit(solution)/shard_map/ppermute | solution.py:10
  19.7 4.5 %collective-permute-start.1 = (bf16[1,7,1,48,128]{4,1,3,2,0:T(8,128)(2,1)}, bf16[1,7,1,48,128]{4,1,3,2,0:T(8,128)(2,1)}, u32[]{:S(2)}, u32[]{:S(2)}) collective-permute-start(bf16[1,7,1,48,128]{4,1,3,2,0:T(8,128)(2,1)} %pad_maximum_fusion.9), channel_id=1, source_target_pairs={{0,8},{8,16},{16,24},{1,9},{9,17},{17,25},{2,10},{10,18},{18,26},{... | collective-permute-start | bytes 258056 | tf_op jit(solution)/shard_map/ppermute | solution.py:10
  24.2 42.8 %all_gather.6 = bf16[3,3,3,16,256]{3,4,2,1,0:T(8,128)(2,1)S(1)} all-gather(bf16[3,3,3,16,8]{3,4,2,1,0:T(8,128)(2,1)S(1)} %copy-done.8), channel_id=1, replica_groups=mesh['sx'=8,'sy'=4,'af'=8] {'sy','af'}, dimensions={4}, use_global_device_ids=true | all-gather | bytes 228096 | tf_op jit(solution)/shard_map/all_gather | solution.py:89
  68.3 2.0 reshape.220
  71.2 2.2 reshape.261
  73.4 21.2 %all-to-all-start.3 = ((bf16[8,2,6912]{2,1,0:T(2,128)(2,1)}), bf16[8,2,6912]{2,1,0:T(2,128)(2,1)S(1)}, u32[]{:S(2)}, u32[]{:S(2)}) async-start(bf16[8,2,6912]{2,1,0:T(2,128)(2,1)} %reshape.261), calls=%async_computation.3 | async-start | bytes 442368 | tf_op jit(solution)/shard_map/all_to_all | solution.py:128
  94.6 1.5 fusion.9
  96.4 2.1 fusion.16
  116.9 1.7 reshape.262
  118.9 2.2 reshape.263
  121.1 3.4 all-to-all-start.4
  126.0 18.7 %all-to-all-done.4 = bf16[4,2,13824]{2,1,0:T(2,128)(2,1)S(1)} async-done(((bf16[4,2,13824]{2,1,0:T(2,128)(2,1)}), bf16[4,2,13824]{2,1,0:T(2,128)(2,1)S(1)}, u32[]{:S(2)}, u32[]{:S(2)}) %all-to-all-start.4) | async-done | bytes 221216 | tf_op jit(solution)/shard_map/all_to_all | solution.py:127
  144.7 1.7 reshape.264
  146.7 2.2 reshape.265
  148.9 5.3 %all-to-all-start.5 = ((bf16[8,2,6912]{2,1,0:T(2,128)(2,1)}), bf16[8,2,6912]{2,1,0:T(2,128)(2,1)}, u32[]{:S(2)}, u32[]{:S(2)}) async-start(bf16[8,2,6912]{2,1,0:T(2,128)(2,1)} %reshape.265), calls=%async_computation.5 | async-start | bytes 442368 | tf_op jit(solution)/shard_map/all_to_all | solution.py:134
  155.0 4.0 %copy.581 = bf16[1,3,6,24,3456]{4,3,2,1,0:T(8,128)(2,1)} copy(bf16[1,3,6,24,3456]{4,1,3,2,0:T(4,128)(2,1)} %slice_dynamic-update-slice_fusion) | data formatting | bytes 5971968 | tf_op jit(solution)/shard_map/concatenate | solution.py:40
  159.0 4.3 %dot_general.205 = bf16[27,128,432]{1,0,2:T(8,128)(2,1)S(1)} reshape(bf16[3456,432]{0,1:T(8,128)(2,1)} %bitcast.438) | data formatting | bytes 5971968 | tf_op jit(solution)/shard_map/dot_general | solution.py:137
  163.3 3.6 %reshape.266 = bf16[8,1,3,4,6,8,24]{6,5,4,3,2,1,0:T(8,128)(2,1)} reshape(bf16[8,2,6912]{2,1,0:T(2,128)(2,1)} %all-to-all-done.5) | data formatting | bytes 442368
  167.0 4.0 %convolution_convert_fusion = bf16[432,256]{1,0:T(8,128)(2,1)} fusion(bf16[432,3456]{1,0:T(8,128)(2,1)} %bitcast.439, bf16[3456,256]{1,0:T(8,128)(2,1)} %bitcast.458), kind=kOutput, calls=%fused_computation.16 | convolution fusion | flops 764522496 | bytes 4976640 | tf_op jit(solution)/shard_map/dot_general | solution.py:102
  171.0 1.8 copy.583
  172.8 2.8 reshape.217
  175.6 2.7 copy.724
  178.3 3.5 reshape.255
  181.8 4.8 %all-to-all-start = ((bf16[8,2,6912]{2,1,0:T(2,128)(2,1)}), bf16[8,2,6912]{2,1,0:T(2,128)(2,1)}, u32[]{:S(2)}, u32[]{:S(2)}) async-start(bf16[8,2,6912]{2,1,0:T(2,128)(2,1)} %reshape.255), calls=%async_computation | async-start | bytes 442368 | tf_op jit(solution)/shard_map/all_to_all | solution.py:106
  189.0 1.6 copy.628
  190.6 2.8 reshape_reshape.4
  193.4 3.6 %reshape.256 = bf16[8,1,3,6,4,8,24]{6,5,4,3,2,1,0:T(8,128)(2,1)} reshape(bf16[8,2,6912]{2,1,0:T(2,128)(2,1)} %all-to-all-done) | data formatting | bytes 442368
  197.0 2.5 fusion.17
  199.5 3.5 reshape.257
  203.0 6.7 %all-to-all-start.1 = ((bf16[8,2,6912]{2,1,0:T(2,128)(2,1)}), bf16[8,2,6912]{2,1,0:T(2,128)(2,1)}, u32[]{:S(2)}, u32[]{:S(2)}) async-start(bf16[8,2,6912]{2,1,0:T(2,128)(2,1)} %reshape.257), calls=%async_computation.1 | async-start | bytes 442368 | tf_op jit(solution)/shard_map/all_to_all | solution.py:108
  209.8 2.3 fusion.6
  212.1 3.9 %copy.631 = f32[32,27,128,8]{2,3,1,0:T(8,128)} copy(f32[32,27,128,8]{2,0,3,1:T(8,128)S(1)} %fusion.6) | data formatting | bytes 7077888 | tf_op jit(solution)/shard_map/transpose | solution.py:142
  216.0 5.1 %all-to-all-done.1 = bf16[8,2,6912]{2,1,0:T(2,128)(2,1)} async-done(((bf16[8,2,6912]{2,1,0:T(2,128)(2,1)}), bf16[8,2,6912]{2,1,0:T(2,128)(2,1)}, u32[]{:S(2)}, u32[]{:S(2)}) %all-to-all-start.1) | async-done | bytes 221216 | tf_op jit(solution)/shard_map/all_to_all | solution.py:108
  221.0 8.0 %all-to-all-start.6 = ((f32[32,27,128,8]{2,3,1,0:T(8,128)}), f32[32,27,128,8]{2,3,1,0:T(8,128)}, u32[]{:S(2)}, u32[]{:S(2)}) async-start(f32[32,27,128,8]{2,3,1,0:T(8,128)} %copy.631), calls=%async_computation.6 | async-start | bytes 7077888 | tf_op jit(solution)/shard_map/all_to_all | solution.py:143
  247.5 1.7 copy.627
  251.0 3.6 %reshape.258 = bf16[8,3,6,4,1,8,24]{6,5,4,3,2,1,0:T(8,128)(2,1)} reshape(bf16[8,2,6912]{2,1,0:T(2,128)(2,1)} %all-to-all-done.1) | data formatting | bytes 442368
  254.7 2.5 copy_bitcast_fusion.10
  257.2 3.5 reshape.259
  260.7 54.5 %all-to-all-done.6 = f32[32,27,128,8]{2,3,1,0:T(8,128)} async-done(((f32[32,27,128,8]{2,3,1,0:T(8,128)}), f32[32,27,128,8]{2,3,1,0:T(8,128)}, u32[]{:S(2)}, u32[]{:S(2)}) %all-to-all-start.6) | async-done | bytes 3538976 | tf_op jit(solution)/shard_map/all_to_all | solution.py:143
  315.2 4.0 %all-to-all-start.2 = ((bf16[4,2,13824]{2,1,0:T(2,128)(2,1)}), bf16[4,2,13824]{2,1,0:T(2,128)(2,1)}, u32[]{:S(2)}, u32[]{:S(2)}) async-start(bf16[4,2,13824]{2,1,0:T(2,128)(2,1)} %reshape.259), calls=%async_computation.2 | async-start | bytes 442368 | tf_op jit(solution)/shard_map/all_to_all | solution.py:107
  319.3 2.2 slice_add_fusion
  325.4 2.8 reduce_sum.18
  330.8 2.2 reshape.267
  333.0 3.6 %all-to-all-start.7 = ((f32[8,1,3456]{2,1,0:T(1,128)}), f32[8,1,3456]{2,1,0:T(1,128)S(1)}, u32[]{:S(2)}, u32[]{:S(2)}) async-start(f32[8,1,3456]{2,1,0:T(1,128)} %reshape.267), calls=%async_computation.7 | async-start | bytes 221184 | tf_op jit(solution)/shard_map/all_to_all | solution.py:146
  339.2 2.9 reshape.260
  343.9 3.2 all-to-all-done.7
  (132 shorter events, 60.7 us)
Async XLA Ops:
  7.2 17.0 %copy-start.8 = (bf16[3,3,3,16,8]{3,4,2,1,0:T(8,128)(2,1)S(1)}, bf16[3,3,3,16,8]{3,4,2,1,0:T(8,128)(2,1)}, u32[]{:S(2)}) copy-start(bf16[3,3,3,16,8]{3,4,2,1,0:T(8,128)(2,1)} %param.4) | copy-start | bytes 20740
  7.2 159.8 %all-gather.2.cloned.1.call-start = ((), (), s32[]{:S(2)}) async-start(), calls=%async_computation.8 | async-start | bytes 1990656 | tf_op jit(solution)/shard_map/all_gather | solution.py:90
  9.3 9.7 %collective-permute-start = (bf16[1,1,12,48,128]{4,1,3,2,0:T(2,128)(2,1)S(1)}, bf16[1,1,12,48,128]{4,1,3,2,0:T(2,128)(2,1)S(1)}, u32[]{:S(2)}, u32[]{:S(2)}) collective-permute-start(bf16[1,1,12,48,128]{4,1,3,2,0:T(2,128)(2,1)S(1)} %slice.315), channel_id=1, source_target_pairs={{0,32},{32,64},{64,96},{96,128},{128,160},{160,192},{192,224},{1,3... | collective-permute-start | bytes 442376 | tf_op jit(solution)/shard_map/ppermute | solution.py:10
  19.0 0.7 copy-start.6
  19.7 74.9 %collective-permute-start.1 = (bf16[1,7,1,48,128]{4,1,3,2,0:T(8,128)(2,1)}, bf16[1,7,1,48,128]{4,1,3,2,0:T(8,128)(2,1)}, u32[]{:S(2)}, u32[]{:S(2)}) collective-permute-start(bf16[1,7,1,48,128]{4,1,3,2,0:T(8,128)(2,1)} %pad_maximum_fusion.9), channel_id=1, source_target_pairs={{0,8},{8,16},{16,24},{1,9},{9,17},{17,25},{2,10},{10,18},{18,26},{... | collective-permute-start | bytes 258056 | tf_op jit(solution)/shard_map/ppermute | solution.py:10
  71.1 23.5 %copy-start.7 = (bf16[1,1,12,48,128]{4,1,3,2,0:T(2,128)(2,1)S(1)}, bf16[1,1,12,48,128]{4,1,3,2,0:T(2,128)(2,1)}, u32[]{:S(2)}) copy-start(bf16[1,1,12,48,128]{4,1,3,2,0:T(2,128)(2,1)} %copy-done.6) | copy-start | bytes 442372
  73.4 43.5 %all-to-all-start.3 = ((bf16[8,2,6912]{2,1,0:T(2,128)(2,1)}), bf16[8,2,6912]{2,1,0:T(2,128)(2,1)S(1)}, u32[]{:S(2)}, u32[]{:S(2)}) async-start(bf16[8,2,6912]{2,1,0:T(2,128)(2,1)} %reshape.261), calls=%async_computation.3 | async-start | bytes 442368 | tf_op jit(solution)/shard_map/all_to_all | solution.py:128
  121.1 23.6 %all-to-all-start.4 = ((bf16[4,2,13824]{2,1,0:T(2,128)(2,1)}), bf16[4,2,13824]{2,1,0:T(2,128)(2,1)S(1)}, u32[]{:S(2)}, u32[]{:S(2)}) async-start(bf16[4,2,13824]{2,1,0:T(2,128)(2,1)} %reshape.263), calls=%async_computation.4 | async-start | bytes 442368 | tf_op jit(solution)/shard_map/all_to_all | solution.py:127
  148.9 14.4 %all-to-all-start.5 = ((bf16[8,2,6912]{2,1,0:T(2,128)(2,1)}), bf16[8,2,6912]{2,1,0:T(2,128)(2,1)}, u32[]{:S(2)}, u32[]{:S(2)}) async-start(bf16[8,2,6912]{2,1,0:T(2,128)(2,1)} %reshape.265), calls=%async_computation.5 | async-start | bytes 442368 | tf_op jit(solution)/shard_map/all_to_all | solution.py:134
  181.8 11.6 %all-to-all-start = ((bf16[8,2,6912]{2,1,0:T(2,128)(2,1)}), bf16[8,2,6912]{2,1,0:T(2,128)(2,1)}, u32[]{:S(2)}, u32[]{:S(2)}) async-start(bf16[8,2,6912]{2,1,0:T(2,128)(2,1)} %reshape.255), calls=%async_computation | async-start | bytes 442368 | tf_op jit(solution)/shard_map/all_to_all | solution.py:106
  188.0 1.0 copy-start.1
  203.0 18.0 %all-to-all-start.1 = ((bf16[8,2,6912]{2,1,0:T(2,128)(2,1)}), bf16[8,2,6912]{2,1,0:T(2,128)(2,1)}, u32[]{:S(2)}, u32[]{:S(2)}) async-start(bf16[8,2,6912]{2,1,0:T(2,128)(2,1)} %reshape.257), calls=%async_computation.1 | async-start | bytes 442368 | tf_op jit(solution)/shard_map/all_to_all | solution.py:108
  216.0 13.0 %copy-start.2 = (bf16[1,3,6,24,4,8,1,8]{3,7,2,4,1,5,6,0:T(8,128)(2,1)S(1)}, bf16[1,3,6,24,4,8,1,8]{3,7,2,4,1,5,6,0:T(8,128)(2,1)}, u32[]{:S(2)}) copy-start(bf16[1,3,6,24,4,8,1,8]{3,7,2,4,1,5,6,0:T(8,128)(2,1)} %copy-done.1) | copy-start | bytes 663556
  221.0 94.2 %all-to-all-start.6 = ((f32[32,27,128,8]{2,3,1,0:T(8,128)}), f32[32,27,128,8]{2,3,1,0:T(8,128)}, u32[]{:S(2)}, u32[]{:S(2)}) async-start(f32[32,27,128,8]{2,3,1,0:T(8,128)} %copy.631), calls=%async_computation.6 | async-start | bytes 7077888 | tf_op jit(solution)/shard_map/all_to_all | solution.py:143
  229.0 1.5 copy-start.5
  249.2 1.6 copy-start
  249.3 69.9 %collective-permute-start.2 = (f32[1,1,13,49,128]{4,1,3,2,0:T(1,128)S(1)}, f32[1,1,13,49,128]{4,1,3,2,0:T(1,128)S(1)}, u32[]{:S(2)}, u32[]{:S(2)}) collective-permute-start(f32[1,1,13,49,128]{4,1,3,2,0:T(1,128)S(1)} %slice.380), channel_id=1, source_target_pairs={{32,0},{64,32},{96,64},{128,96},{160,128},{192,160},{224,192},{33,... | collective-permute-start | bytes 978440 | tf_op jit(solution)/shard_map/ppermute | solution.py:10
  315.2 17.8 %all-to-all-start.2 = ((bf16[4,2,13824]{2,1,0:T(2,128)(2,1)}), bf16[4,2,13824]{2,1,0:T(2,128)(2,1)}, u32[]{:S(2)}, u32[]{:S(2)}) async-start(bf16[4,2,13824]{2,1,0:T(2,128)(2,1)} %reshape.259), calls=%async_computation.2 | async-start | bytes 442368 | tf_op jit(solution)/shard_map/all_to_all | solution.py:107
  321.5 0.7 copy-start.4
  322.9 13.7 %collective-permute-start.3 = (bf16[1,6,1,49,128]{4,1,3,2,0:T(8,128)(2,1)}, bf16[1,6,1,49,128]{4,1,3,2,0:T(8,128)(2,1)}, u32[]{:S(2)}, u32[]{:S(2)}) collective-permute-start(bf16[1,6,1,49,128]{4,1,3,2,0:T(8,128)(2,1)} %slice.384), channel_id=1, source_target_pairs={{8,0},{16,8},{24,16},{9,1},{17,9},{25,17},{10,2},{18,10},{26,18},{... | collective-permute-start | bytes 225800 | tf_op jit(solution)/shard_map/ppermute | solution.py:10
  333.0 14.1 %all-to-all-start.7 = ((f32[8,1,3456]{2,1,0:T(1,128)}), f32[8,1,3456]{2,1,0:T(1,128)S(1)}, u32[]{:S(2)}, u32[]{:S(2)}) async-start(f32[8,1,3456]{2,1,0:T(1,128)} %reshape.267), calls=%async_computation.7 | async-start | bytes 221184 | tf_op jit(solution)/shard_map/all_to_all | solution.py:146
  336.6 1.3 copy-start.3
Sparse Core Ops, SparseCore 0:
  68.4 87.4 all-gather.1
